TPU v7x, 32 devices: a whole 2x2x4 slice. The times are simulated.
32 devices in a mesh: dp: 8 (over z, y), col: 4 (over x, core).
Axes of the slice: x: 2, y: 2, z: 4, core: 2. Of those that a mesh axis runs over, the one named last changes fastest.
Arguments:
- tokens: bfloat16 [8192, 8192], P('dp', 'col'), may hold values from -6 to 6
- out_grad: bfloat16 [8192, 8192], P(('dp', 'col')), may hold values from -6 to 6
- weight: float32 [8192, 8192], P('dp', 'col'), may hold values from -6 to 6
- second: float32 [8192, 8192], P('dp', 'col'), may hold values from 0.0001 to 0.001
- momentum: float32 [8192, 512], P(('dp', 'col')), may hold values from -0.12 to 0.12
- sign_seed: int32 [1], replicated, may hold values from 0 to 999999
- step_number: int32 [1], replicated, may hold values from 1 to 999999
Outputs:
- new_weight: float32 [8192, 8192], P('dp', 'col')
- new_second: float32 [8192, 8192], P('dp', 'col')
- new_momentum: float32 [8192, 512], P(('dp', 'col'))
All inputs are finite; a program needn't handle non-finite values.
Results may differ from a plain program's by a relative error of at most 0.00097.
Values may be sent and summed in bfloat16 or wider, within the bound.
No kernel may reach another device: no remote copies, remote signals or barrier semaphores. Data moves between devices by JAX's collectives and lax.ppermute only.
A program may use at most 128 MiB of HBM per device.

v0:
```python
import jax
import jax.numpy as jnp
from jax import lax
from jax.sharding import PartitionSpec as P


def sign_table(sign_seed, step_number, first_row, row_count, low_rank):
    row_ids = first_row + lax.iota(jnp.int32, row_count)
    col_ids = lax.iota(jnp.int32, low_rank)
    flat_index = row_ids[:, None] * low_rank + col_ids[None, :]
    hashed = flat_index * 747796405 + sign_seed[0] * 1664525 + step_number[0] * 1013904223
    hashed = hashed ^ hashed >> 16 & 65535
    hashed = hashed * 2127912213
    hashed = hashed ^ hashed >> 13 & 524287
    hashed = hashed * 1103515245
    hashed = hashed ^ hashed >> 16 & 65535
    low_bit = hashed >> 20 & 1
    return (1 - 2 * low_bit).astype(jnp.float32)


def contract(left_rows, right_rows):
    return lax.dot_general(
        left_rows, right_rows, (((0,), (0,)), ((), ())), preferred_element_type=jnp.float32
    )


def per_device(tokens, out_grad, weight, second, momentum, sign_seed, step_number):
    local_tokens, din_local = tokens.shape
    low_rank = momentum.shape[1]
    owner_rows = momentum.shape[0]
    inv_root = 1.0 / jnp.sqrt(jnp.float32(low_rank))
    col_position = lax.axis_index("col")
    sign_block = sign_table(sign_seed, step_number, col_position * din_local, din_local, low_rank)
    partial_sketch = (
        jnp.dot(tokens, sign_block.astype(jnp.bfloat16), preferred_element_type=jnp.float32)
        * inv_root
    )
    quarter = lax.psum_scatter(partial_sketch, "col", scatter_dimension=0, tiled=True)
    sketch = quarter.astype(jnp.bfloat16)
    total_tokens = lax.axis_size("dp") * local_tokens
    data_count = lax.axis_size("dp")
    col_count = lax.axis_size("col")
    quarter_rows = out_grad.shape[0]
    grouped = out_grad.reshape(quarter_rows, data_count, col_count, owner_rows)
    grouped = jnp.transpose(grouped, (0, 2, 1, 3)).reshape(
        quarter_rows, col_count, data_count * owner_rows
    )
    regrouped = lax.all_to_all(grouped, "col", split_axis=1, concat_axis=0, tiled=True)
    regrouped = regrouped.reshape(quarter_rows * col_count, data_count * owner_rows)
    shard_sketch = lax.all_gather(sketch, "col", axis=0, tiled=True)
    projected = lax.psum_scatter(
        contract(regrouped, shard_sketch), "dp", scatter_dimension=0, tiled=True
    )
    projected = projected / jnp.float32(total_tokens)
    new_momentum = 0.8 * momentum + 0.2 * projected
    row_block = lax.all_gather(new_momentum, "col", axis=0, tiled=True)
    dense_grad = (
        lax.dot_general(
            row_block,
            sign_block,
            (((1,), (1,)), ((), ())),
            precision=lax.Precision.HIGHEST,
            preferred_element_type=jnp.float32,
        )
        * inv_root
    )
    new_second = 0.95 * second + 0.05 * dense_grad * dense_grad
    new_weight = weight - 0.5 * dense_grad / (jnp.sqrt(new_second) + 1e-08)
    return (new_weight, new_second, new_momentum)


def solution(mesh):
    placed = (
        P("dp", "col"),
        P(("dp", "col"), None),
        P("dp", "col"),
        P("dp", "col"),
        P(("dp", "col"), None),
        P(),
        P(),
    )
    return jax.shard_map(
        per_device,
        mesh=mesh,
        in_specs=placed,
        out_specs=(P("dp", "col"), P("dp", "col"), P(("dp", "col"), None)),
        check_vma=False,
    )
```

profile of v0, /device:TPU:0, one launch (start us, length us, event | category | flops | bytes accessed | tf_op | source)
XLA Modules:
  0.0 263.5 jit_solution(1373859997120523536)
XLA Ops:
  7.2 0.0 reduce-scatter.3.cloned.1.call-start
  8.5 7.7 %multiply_bitcast_fusion = f32[1024,512]{0,1:T(8,128)} fusion(bf16[1024,2048]{1,0:T(8,128)(2,1)} %param.7, s32[]{:T(128)} %bitcast.1, s32[]{:T(128)} %bitcast, s32[2048]{0:T(1024)S(1)} %add_multiply_fusion), kind=kOutput, calls=%fused_computation.9 | convolution fusion | flops 2170028032 | bytes 6299656 | tf_op jit(solution)/shard_map/dot_general | solution.py:35
  16.2 0.0 reduce-scatter.3.cloned.1.call-update
  16.3 7.8 %reshape.26 = bf16[256,8,4,256]{3,2,1,0:T(4,128)(2,1)} reshape(bf16[256,8192]{1,0:T(8,128)(2,1)} %param.8) | data formatting | bytes 8388608 | tf_op jit(solution)/shard_map/reshape | solution.py:44
  24.1 4.9 %copy.16 = bf16[256,8,4,256]{3,1,0,2:T(8,128)(2,1)} copy(bf16[256,8,4,256]{3,2,1,0:T(4,128)(2,1)} %reshape.26) | data formatting | bytes 8388608 | tf_op jit(solution)/shard_map/reshape | solution.py:44
  29.0 7.4 %reshape.27 = bf16[256,4,2048]{2,0,1:T(8,128)(2,1)} reshape(bf16[256,4,8,256]{3,2,0,1:T(8,128)(2,1)} %bitcast.22) | data formatting | bytes 8388608 | tf_op jit(solution)/shard_map/reshape | solution.py:45
  36.3 4.8 %all-to-all-start = ((bf16[256,4,2048]{2,0,1:T(8,128)(2,1)}), bf16[256,4,2048]{2,0,1:T(8,128)(2,1)}, u32[]{:S(2)}, u32[]{:S(2)}) async-start(bf16[256,4,2048]{2,0,1:T(8,128)(2,1)} %reshape.27), calls=%async_computation.1 | async-start | bytes 8388608 | tf_op jit(solution)/shard_map/all_to_all | solution.py:48
  41.2 0.0 all-gather.3.cloned.1.call-start
  41.2 12.6 %reduce-scatter.3.cloned.1.call-done = f32[256,512]{0,1:T(8,128)} async-done(((f32[1024,512]{0,1:T(8,128)}), f32[256,512]{0,1:T(8,128)}) %reduce-scatter.3.cloned.1.call-update) | async-done | bytes 524304 | tf_op jit(solution)/shard_map/reduce_scatter | solution.py:38
  53.8 1.8 convert_element_type.11
  55.6 0.0 all-gather.3.cloned.1.call-update
  55.6 0.0 reduce-scatter.5.cloned.1.call-start
  55.7 44.1 %all-to-all-done = bf16[256,4,2048]{2,0,1:T(8,128)(2,1)} async-done(((bf16[256,4,2048]{2,0,1:T(8,128)(2,1)}), bf16[256,4,2048]{2,0,1:T(8,128)(2,1)}, u32[]{:S(2)}, u32[]{:S(2)}) %all-to-all-start) | async-done | bytes 4194336 | tf_op jit(solution)/shard_map/all_to_all | solution.py:48
  99.7 0.0 all-gather.3.cloned.1.call-done
  99.7 6.9 %convolution_bitcast_fusion = f32[2048,512]{0,1:T(8,128)} fusion(bf16[1024,512]{0,1:T(8,128)(2,1)} %all-gather.3.cloned.1.call-done, bf16[1024,2048]{1,0:T(8,128)(2,1)} %bitcast.6), kind=kOutput, calls=%fused_computation.7 | convolution fusion | flops 2147483648 | bytes 9437184 | tf_op jit(solution)/shard_map/dot_general | solution.py:22
  106.6 0.0 copy-start
  106.6 0.0 reduce-scatter.5.cloned.1.call-update
  106.6 0.2 all-gather.5.cloned.1.call-start
  106.9 0.8 copy-done
  107.6 0.2 copy.12
  107.8 87.7 %reduce-scatter.5.cloned.1.call-done = f32[256,512]{0,1:T(8,128)} async-done(((f32[2048,512]{0,1:T(8,128)}), f32[256,512]{0,1:T(8,128)}) %reduce-scatter.5.cloned.1.call-update) | async-done | bytes 524304 | tf_op jit(solution)/shard_map/reduce_scatter | solution.py:51
  195.5 1.9 multiply_add_fusion.1
  197.5 0.0 all-gather.5.cloned.1.call-update
  197.5 2.0 copy.14
  199.5 20.3 %all-gather.5.cloned.1.call-done = f32[1024,512]{0,1:T(8,128)} async-done(((f32[256,512]{0,1:T(8,128)}), f32[1024,512]{0,1:T(8,128)}) %all-gather.5.cloned.1.call-update) | async-done | bytes 2097168 | tf_op jit(solution)/shard_map/all_gather | solution.py:56
  219.8 37.1 %divide_subtract_fusion = (f32[1024,2048]{1,0:T(8,128)}, f32[1024,2048]{1,0:T(8,128)}) fusion(f32[1024,2048]{1,0:T(8,128)} %param.9, f32[1024,2048]{1,0:T(8,128)} %param.10, f32[1024,512]{0,1:T(8,128)} %all-gather.5.cloned.1.call-done, s32[]{:T(128)} %bitcast.1, s32[]{:T(128)} %bitcast, s32[2048]{0:T(1024)S(1)} %add_multiply_fusion), kind=kOutput, calls=%fused_computation | convolution fusion | flops 12924747776 | bytes 35659784 | tf_op jit(solution)/shard_map/dot_general | solution.py:58
  (1 shorter events, 0.0 us)
Async XLA Ops:
  7.2 46.7 %reduce-scatter.3.cloned.1.call-start = ((), (), s32[]{:S(2)}) async-start(), calls=%async_computation.3 | async-start | bytes 2621440 | tf_op jit(solution)/shard_map/reduce_scatter | solution.py:38
  36.3 63.4 %all-to-all-start = ((bf16[256,4,2048]{2,0,1:T(8,128)(2,1)}), bf16[256,4,2048]{2,0,1:T(8,128)(2,1)}, u32[]{:S(2)}, u32[]{:S(2)}) async-start(bf16[256,4,2048]{2,0,1:T(8,128)(2,1)} %reshape.27), calls=%async_computation.1 | async-start | bytes 8388608 | tf_op jit(solution)/shard_map/all_to_all | solution.py:48
  41.2 58.5 %all-gather.3.cloned.1.call-start = ((), (), s32[]{:S(2)}) async-start(), calls=%async_computation.4 | async-start | bytes 1310720 | tf_op jit(solution)/shard_map/all_gather | solution.py:50
  55.6 139.9 %reduce-scatter.5.cloned.1.call-start = ((), (), s32[]{:S(2)}) async-start(), calls=%async_computation.5 | async-start | bytes 4718592 | tf_op jit(solution)/shard_map/reduce_scatter | solution.py:51
  106.6 1.0 copy-start
  106.6 113.2 %all-gather.5.cloned.1.call-start = ((), (), s32[]{:S(2)}) async-start(), calls=%async_computation.6 | async-start | bytes 2621440 | tf_op jit(solution)/shard_map/all_gather | solution.py:56
Sparse Core Ops, SparseCore 0:
  16.4 37.4 reduce-scatter.2
  56.0 21.9 all-gather.2
  106.7 88.7 reduce-scatter.4
  197.6 22.1 all-gather.4
where the time goes:
time: 264 us; the launch traced here: 263 us
  waiting for transfers between devices  165 us (62%)
  matrix products  51.7 us (20%)
  local copies, waits for them, and re-layouts  23.1 us (9%)
  between operations  15.1 us (6%)
  starting transfers between devices  5.19 us (2%)
  other arithmetic  3.69 us (1%)
    reduce_scatter x1, waiting for transfers between devices, per_device(): lax.psum_scatter(contract(regrouped, shard_sketch), 'dp', scatter_dimensi...  87.7 us
    all_to_all x1, waiting for transfers between devices, per_device(): lax.all_to_all(grouped, 'col', split_axis=1, concat_axis=0, tiled=True)  44.1 us
    dot_general x1, matrix products, per_device(): lax.dot_general(row_block, sign_block, (((1,), (1,)), ((), ())), precisio...  37.1 us
    all_gather x1, waiting for transfers between devices, per_device(): row_block = lax.all_gather(new_momentum, 'col', axis=0, tiled=True)  20.3 us
    reshape x2, local copies, waits for them, and re-layouts, per_device(): grouped = out_grad.reshape(quarter_rows, data_count, col_count, owner_rows)  12.7 us
    reduce_scatter x1, waiting for transfers between devices, per_device(): lax.psum_scatter(partial_sketch, 'col', scatter_dimension=0, tiled=True)  12.6 us
    dot_general x1, matrix products, per_device(): jnp.dot(tokens, sign_block.astype(jnp.bfloat16), preferred_element_type=j...  7.71 us
    reshape x1, local copies, waits for them, and re-layouts, per_device(): jnp.transpose(grouped, (0, 2, 1, 3))  7.37 us
  transfers between devices with their start and end apart: 5, of which 4 were waited for; matrix products, arithmetic and copies ran while one was open for 9% of the time, Pallas kernels for 0%

commit v1 on v0

--- a/solution.py
+++ b/solution.py
@@ -2,6 +2,12 @@
 import jax.numpy as jnp
 from jax import lax
 from jax.sharding import PartitionSpec as P
+
+
+def stacked_exchange(array, axis, split, join):
+    cells = jnp.split(array, lax.axis_size(axis), axis=split)
+    received = lax.all_to_all(jnp.stack(cells), axis, 0, 0)
+    return jnp.concatenate(received, axis=join)
 
 
 def sign_table(sign_seed, step_number, first_row, row_count, low_rank):
@@ -45,7 +51,7 @@
     grouped = jnp.transpose(grouped, (0, 2, 1, 3)).reshape(
         quarter_rows, col_count, data_count * owner_rows
     )
-    regrouped = lax.all_to_all(grouped, "col", split_axis=1, concat_axis=0, tiled=True)
+    regrouped = stacked_exchange(grouped, "col", 1, 0)
     regrouped = regrouped.reshape(quarter_rows * col_count, data_count * owner_rows)
     shard_sketch = lax.all_gather(sketch, "col", axis=0, tiled=True)
     projected = lax.psum_scatter(

time: 264 us -> 255 us (0.966)
  matrix products: 51.7 us -> 40.2 us
    dot_general x1, matrix products: 37.1 us -> 25.6 us  [per_device(): lax.dot_general(row_block, sign_block, (((1,), (1,)), ((), ())), precisio...]
    reduce_scatter x1, waiting for transfers between devices: 12.6 us -> 4.02 us  [per_device(): lax.psum_scatter(partial_sketch, 'col', scatter_dimension=0, tiled=True)]
    all_to_all x1, waiting for transfers between devices: 44.1 us -> 49 us  [stacked_exchange(): received = lax.all_to_all(jnp.stack(cells), axis, 0, 0)]
    unnamed x4 -> x2, local copies, waits for them, and re-layouts: 3.02 us -> 0.01 us
    another operation x0 -> x1, local copies, waits for them, and re-layouts: none -> 2.75 us  [stacked_exchange(): received = lax.all_to_all(jnp.stack(cells), axis, 0, 0)]
  transfers between devices with their start and end apart: 5 -> 5, of which waited for: 4 -> 4; matrix products, arithmetic and copies ran while one was open for 9% -> 11% of each run, Pallas kernels for 0% -> 0%
where the time goes in v1:
time: 255 us; the launch traced here: 254 us
  waiting for transfers between devices  165 us (65%)
  matrix products  40.2 us (16%)
  local copies, waits for them, and re-layouts  22.8 us (9%)
  between operations  15.1 us (6%)
  other arithmetic  6.01 us (2%)
  starting transfers between devices  5.18 us (2%)
    reduce_scatter x1, waiting for transfers between devices, per_device(): lax.psum_scatter(contract(regrouped, shard_sketch), 'dp', scatter_dimensi...  89.2 us
    all_to_all x1, waiting for transfers between devices, stacked_exchange(): received = lax.all_to_all(jnp.stack(cells), axis, 0, 0)  49 us
    dot_general x1, matrix products, per_device(): lax.dot_general(row_block, sign_block, (((1,), (1,)), ((), ())), precisio...  25.6 us
    all_gather x1, waiting for transfers between devices, per_device(): row_block = lax.all_gather(new_momentum, 'col', axis=0, tiled=True)  22.4 us
    reshape x2, local copies, waits for them, and re-layouts, per_device(): grouped = out_grad.reshape(quarter_rows, data_count, col_count, owner_rows)  12.7 us
    dot_general x1, matrix products, per_device(): jnp.dot(tokens, sign_block.astype(jnp.bfloat16), preferred_element_type=j...  7.71 us
    reshape x1, local copies, waits for them, and re-layouts, per_device(): jnp.transpose(grouped, (0, 2, 1, 3))  7.37 us
    dot_general x1, matrix products, contract(): lax.dot_general(left_rows, right_rows, (((0,), (0,)), ((), ())), preferre...  6.9 us
  transfers between devices with their start and end apart: 5, of which 4 were waited for; matrix products, arithmetic and copies ran while one was open for 11% of the time, Pallas kernels for 0%

profile of v1, /device:TPU:0, one launch (start us, length us, event | category | flops | bytes accessed | tf_op | source)
XLA Modules:
  0.0 254.0 jit_solution(12626370248299274747)
XLA Ops:
  7.2 0.0 reduce-scatter.3.cloned.1.call-start
  8.5 7.7 %multiply_bitcast_fusion = f32[1024,512]{0,1:T(8,128)} fusion(bf16[1024,2048]{1,0:T(8,128)(2,1)} %param.7, s32[]{:T(128)} %bitcast.7, s32[]{:T(128)} %bitcast.6, s32[2048]{0:T(1024)S(1)} %add_multiply_fusion), kind=kOutput, calls=%fused_computation.9 | convolution fusion | flops 2170028032 | bytes 6299656 | tf_op jit(solution)/shard_map/dot_general | solution.py:41
  16.2 0.0 reduce-scatter.3.cloned.1.call-update
  16.3 7.8 %reshape.22 = bf16[256,8,4,256]{3,2,1,0:T(4,128)(2,1)} reshape(bf16[256,8192]{1,0:T(8,128)(2,1)} %param.8) | data formatting | bytes 8388608 | tf_op jit(solution)/shard_map/reshape | solution.py:50
  24.1 4.9 %copy.15 = bf16[256,8,4,256]{3,1,0,2:T(8,128)(2,1)} copy(bf16[256,8,4,256]{3,2,1,0:T(4,128)(2,1)} %reshape.22) | data formatting | bytes 8388608 | tf_op jit(solution)/shard_map/reshape | solution.py:50
  29.0 7.4 %reshape.23 = bf16[256,4,2048]{2,0,1:T(8,128)(2,1)} reshape(bf16[256,4,8,256]{3,2,0,1:T(8,128)(2,1)} %bitcast.24) | data formatting | bytes 8388608 | tf_op jit(solution)/shard_map/reshape | solution.py:51
  36.3 2.7 %slice_bitcast_fusion.3 = (bf16[1,256,1,2048]{3,1,2,0:T(8,128)(2,1)S(1)}, bf16[1,256,1,2048]{3,1,2,0:T(8,128)(2,1)S(1)}, bf16[1,256,1,2048]{3,1,2,0:T(8,128)(2,1)S(1)}, bf16[1,256,1,2048]{3,1,2,0:T(8,128)(2,1)S(1)}) fusion(bf16[256,4,2048]{2,0,1:T(8,128)(2,1)} %reshape.23), kind=kLoop, calls=%fused_computation.13 | loop fusion | bytes 8388608 | tf_op jit(solution)/shard_map/stack | solution.py:9
  39.1 2.3 pad_maximum_fusion
  41.4 4.8 %all-to-all-start = ((bf16[4,256,1,2048]{3,1,2,0:T(8,128)(2,1)}), bf16[4,256,1,2048]{3,1,2,0:T(8,128)(2,1)}, u32[]{:S(2)}, u32[]{:S(2)}) async-start(bf16[4,256,1,2048]{3,1,2,0:T(8,128)(2,1)} %pad_maximum_fusion), calls=%async_computation | async-start | bytes 8388608 | tf_op jit(solution)/shard_map/all_to_all | solution.py:9
  46.2 0.0 all-gather.3.cloned.1.call-start
  46.3 4.0 %reduce-scatter.3.cloned.1.call-done = f32[256,512]{0,1:T(8,128)} async-done(((f32[1024,512]{0,1:T(8,128)}), f32[256,512]{0,1:T(8,128)}) %reduce-scatter.3.cloned.1.call-update) | async-done | bytes 524304 | tf_op jit(solution)/shard_map/reduce_scatter | solution.py:44
  50.3 1.8 convert_element_type.11
  52.1 0.0 all-gather.3.cloned.1.call-update
  52.1 0.0 reduce-scatter.5.cloned.1.call-start
  52.1 49.0 %all-to-all-done = bf16[4,256,1,2048]{3,1,2,0:T(8,128)(2,1)} async-done(((bf16[4,256,1,2048]{3,1,2,0:T(8,128)(2,1)}), bf16[4,256,1,2048]{3,1,2,0:T(8,128)(2,1)}, u32[]{:S(2)}, u32[]{:S(2)}) %all-to-all-start) | async-done | bytes 4194336 | tf_op jit(solution)/shard_map/all_to_all | solution.py:9
  101.2 0.0 all-gather.3.cloned.1.call-done
  101.2 6.9 %fusion.23 = f32[2048,512]{1,0:T(8,128)} fusion(bf16[1024,2048]{1,0:T(8,128)(2,1)} %bitcast.5, bf16[1024,512]{0,1:T(8,128)(2,1)} %all-gather.3.cloned.1.call-done), kind=kOutput, calls=%fused_computation.36 | convolution fusion | flops 2147483648 | bytes 9437184 | tf_op jit(solution)/shard_map/dot_general | solution.py:28
  108.1 0.0 copy-start
  108.1 0.0 reduce-scatter.5.cloned.1.call-update
  108.1 0.2 all-gather.5.cloned.1.call-start
  108.3 89.2 %reduce-scatter.5.cloned.1.call-done = f32[256,512]{1,0:T(8,128)} async-done(((f32[2048,512]{1,0:T(8,128)}), f32[256,512]{1,0:T(8,128)}) %reduce-scatter.5.cloned.1.call-update) | async-done | bytes 524304 | tf_op jit(solution)/shard_map/reduce_scatter | solution.py:57
  197.6 0.0 copy-done
  197.6 1.9 multiply_add_fusion.1
  199.5 0.0 all-gather.5.cloned.1.call-update
  199.5 22.4 %all-gather.5.cloned.1.call-done = f32[1024,512]{1,0:T(8,128)} async-done(((f32[256,512]{1,0:T(8,128)}), f32[1024,512]{1,0:T(8,128)}) %all-gather.5.cloned.1.call-update) | async-done | bytes 2097168 | tf_op jit(solution)/shard_map/all_gather | solution.py:62
  221.9 25.6 %divide_subtract_fusion = (f32[1024,2048]{1,0:T(8,128)}, f32[1024,2048]{1,0:T(8,128)}) fusion(f32[1024,2048]{1,0:T(8,128)} %param.9, f32[1024,2048]{1,0:T(8,128)} %param.10, f32[1024,512]{1,0:T(8,128)} %all-gather.5.cloned.1.call-done, s32[]{:T(128)} %bitcast.7, s32[]{:T(128)} %bitcast.6, s32[2048]{0:T(1024)S(1)} %add_multiply_fusion), kind=kOutput, calls=%fused_computation | convolution fusion | flops 12924747776 | bytes 35659784 | tf_op jit(solution)/shard_map/dot_general | solution.py:64
  (1 shorter events, 0.0 us)
Async XLA Ops:
  7.2 43.1 %reduce-scatter.3.cloned.1.call-start = ((), (), s32[]{:S(2)}) async-start(), calls=%async_computation.3 | async-start | bytes 2621440 | tf_op jit(solution)/shard_map/reduce_scatter | solution.py:44
  41.4 59.8 %all-to-all-start = ((bf16[4,256,1,2048]{3,1,2,0:T(8,128)(2,1)}), bf16[4,256,1,2048]{3,1,2,0:T(8,128)(2,1)}, u32[]{:S(2)}, u32[]{:S(2)}) async-start(bf16[4,256,1,2048]{3,1,2,0:T(8,128)(2,1)} %pad_maximum_fusion), calls=%async_computation | async-start | bytes 8388608 | tf_op jit(solution)/shard_map/all_to_all | solution.py:9
  46.2 55.0 %all-gather.3.cloned.1.call-start = ((), (), s32[]{:S(2)}) async-start(), calls=%async_computation.4 | async-start | bytes 1310720 | tf_op jit(solution)/shard_map/all_gather | solution.py:56
  52.1 145.5 %reduce-scatter.5.cloned.1.call-start = ((), (), s32[]{:S(2)}) async-start(), calls=%async_computation.5 | async-start | bytes 4718592 | tf_op jit(solution)/shard_map/reduce_scatter | solution.py:57
  108.1 89.5 %copy-start = (f32[256,512]{1,0:T(8,128)S(1)}, f32[256,512]{1,0:T(8,128)}, u32[]{:S(2)}) copy-start(f32[256,512]{1,0:T(8,128)} %param.11) | copy-start | bytes 1572868
  108.1 113.8 %all-gather.5.cloned.1.call-start = ((), (), s32[]{:S(2)}) async-start(), calls=%async_computation.6 | async-start | bytes 2621440 | tf_op jit(solution)/shard_map/all_gather | solution.py:62
Sparse Core Ops, SparseCore 0:
  16.4 33.8 reduce-scatter.2
  52.4 22.7 all-gather.2
  108.2 89.2 reduce-scatter.4
  199.6 22.1 all-gather.4
